TPU v7x, 256 devices: a whole 4x4x8 slice. The times are simulated.
256 devices in a mesh: grp: 4 (over y), dom: 64 (over x, z, core).
Axes of the slice: x: 4, y: 4, z: 8, core: 2. Of those that a mesh axis runs over, the one named last changes fastest.
Arguments:
- features: bfloat16 [786432, 256], P(('grp', 'dom')), may hold values from -6 to 6
- boundary_cache: float32 [65536, 256], P(('grp', 'dom')), may hold values from -6 to 6
- adjacency: bfloat16 [6144, 2, 128, 128], P(('grp', 'dom')), may hold values from -0.375 to 0.375
- neighbor: int32 [6144, 2], P(('grp', 'dom')), may hold values from 0 to 87
- counts: int32 [6144], P(('grp', 'dom')), may hold values from 1 to 2
- wanted: int32 [256, 64], P(('grp', 'dom')), may hold values from 0 to 1
- weight_in: bfloat16 [512, 512], replicated, may hold values from -0.25 to 0.25
- weight_out: bfloat16 [512, 256], replicated, may hold values from -0.25 to 0.25
- cotangent: bfloat16 [786432, 256], P(('grp', 'dom')), may hold values from -6 to 6
Outputs:
- grad_features: bfloat16 [786432, 256], P(('grp', 'dom'))
- grad_weight_in: float32 [512, 512], P('dom')
- grad_weight_out: float32 [512, 256], P('dom')
Inputs may be any that keep to these rules, and one draw needn't show every extreme that they name: `neighbor`: A value under 24 names a block of the same partition; a value 24 + q names the boundary block that the partition reads from partition q of its group. Slots from counts[b] on are padding and carry no edges.
All inputs are finite; a program needn't handle non-finite values.
Results may differ from a plain program's by a relative error of at most 0.0054.
Values may be sent and summed in bfloat16 or wider, within the bound.
No kernel may reach another device: no remote copies, remote signals or barrier semaphores. Data moves between devices by JAX's collectives and lax.ppermute only.
A program may use at most 128 MiB of HBM per device.

v0:
```python
import math
import jax
import jax.numpy as jnp
from jax import lax
from jax.sharding import PartitionSpec as P


def local(
    features, boundary_cache, adjacency, neighbor, counts, wanted, weight_in, weight_out, cotangent
):
    nblocks = adjacency.shape[0]
    slot_total = adjacency.shape[1]
    block_rows = adjacency.shape[2]
    channels = features.shape[1]
    node_rows = nblocks * block_rows
    partners = lax.axis_size("dom")
    cache_copy = boundary_cache.astype(jnp.bfloat16)
    exported = cache_copy.reshape(-1, block_rows, channels)
    export_total = exported.shape[0]
    exported_all = lax.all_gather(cache_copy, "dom", axis=0, tiled=True).reshape(
        partners, export_total, block_rows, channels
    )
    selected = wanted[0]
    boundary = exported_all[:, 0]
    boundary = jnp.where((selected == 1)[:, None, None], exported_all[:, 1], boundary)
    owned = features.reshape(nblocks, block_rows, channels)
    sources = jnp.concatenate([owned, boundary], 0)
    active = jnp.arange(slot_total)[None, :] < counts[:, None]
    chosen = sources[neighbor]
    chosen = jnp.where(active[:, :, None, None], chosen, jnp.zeros_like(chosen))
    aggregate = jnp.einsum("bsij,bsjf->bif", adjacency, chosen, preferred_element_type=jnp.float32)
    aggregate = aggregate.astype(jnp.bfloat16).reshape(node_rows, channels)
    joined = jnp.concatenate([aggregate, features], 1)
    preact = jnp.dot(joined, weight_in, preferred_element_type=jnp.float32)
    gating = jax.nn.sigmoid(preact)
    hidden = (preact * gating).astype(jnp.bfloat16)
    grad_hidden = jnp.einsum("nf,hf->nh", cotangent, weight_out, preferred_element_type=jnp.float32)
    grad_preact = (grad_hidden * gating * (1.0 + preact * (1.0 - gating))).astype(jnp.bfloat16)
    grad_joined = jnp.einsum(
        "nh,ch->nc", grad_preact, weight_in, preferred_element_type=jnp.float32
    )
    grad_aggregate = (
        grad_joined[:, :channels].astype(jnp.bfloat16).reshape(nblocks, block_rows, channels)
    )
    backward = jnp.einsum(
        "bsji,bjf->bsif", adjacency, grad_aggregate, preferred_element_type=jnp.float32
    )
    local_hit = active & (neighbor < nblocks)
    routing = (neighbor[None, :, :] == jnp.arange(nblocks)[:, None, None]) & local_hit[None]
    spread = jnp.einsum(
        "cbs,bsif->cif", routing.astype(jnp.float32), backward, precision=lax.Precision.HIGHEST
    )
    grad_features = (grad_joined[:, channels:] + spread.reshape(node_rows, channels)).astype(
        jnp.bfloat16
    )
    node_total = node_rows * lax.axis_size("grp") * partners
    loss_scale = 1.0 / math.sqrt(node_total)
    rows_in = weight_in.shape[0] // partners
    rows_out = weight_out.shape[0] // partners
    summed = lax.psum(
        (
            jnp.einsum("nc,nh->ch", joined, grad_preact, preferred_element_type=jnp.float32)
            * loss_scale,
            jnp.einsum("nh,nf->hf", hidden, cotangent, preferred_element_type=jnp.float32)
            * loss_scale,
        ),
        ("grp", "dom"),
    )
    position = lax.axis_index("dom")
    grad_weight_in = lax.dynamic_slice_in_dim(summed[0], position * rows_in, rows_in, 0)
    grad_weight_out = lax.dynamic_slice_in_dim(summed[1], position * rows_out, rows_out, 0)
    return (grad_features, grad_weight_in, grad_weight_out)


def solution(mesh):
    in_specs = (
        P(("grp", "dom"), None),
        P(("grp", "dom"), None),
        P(("grp", "dom"), None, None, None),
        P(("grp", "dom"), None),
        P(("grp", "dom")),
        P(("grp", "dom"), None),
        P(),
        P(),
        P(("grp", "dom"), None),
    )
    out_specs = (P(("grp", "dom"), None), P("dom", None), P("dom", None))
    return jax.shard_map(local, mesh=mesh, in_specs=in_specs, out_specs=out_specs, check_vma=False)
```

profile of v0, /device:TPU:2, one launch (start us, length us, event | category | flops | bytes accessed | tf_op | source)
XLA Modules:
  0.0 416.0 jit_solution(14826898906315317452)
XLA Ops:
  7.2 1.7 convert_element_type.20
  9.0 0.7 compare_and_fusion
  9.8 0.7 compare_select_fusion
  10.7 0.7 compare_bitcast_fusion
  11.4 84.6 %all-gather.2.cloned.1.call-done = bf16[16384,256]{1,0:T(8,128)(2,1)} async-done(((bf16[256,256]{1,0:T(8,128)(2,1)}), bf16[16384,256]{1,0:T(8,128)(2,1)}) %all-gather.2.cloned.1.call-update) | async-done | bytes 8388624 | tf_op jit(solution)/shard_map/all_gather | solution.py:20
  96.0 3.9 fusion.2
  99.9 3.0 pad_maximum_fusion
  102.9 5.2 %gather_fusion = bf16[48,128,256]{2,1,0:T(8,128)(2,1)} fusion(bf16[88,128,256]{2,1,0:T(8,128)(2,1)} %pad_maximum_fusion, s32[1024]{0:T(1024)S(1)} %pad_clamp_fusion), kind=kCustom, calls=%fused_computation | custom fusion | bytes 6291648 | tf_op jit(solution)/shard_map/gather | solution.py:29
  108.1 2.6 bitcast_convert_fusion
  110.8 1.8 fusion.9
  112.6 2.6 fusion.17
  115.2 2.7 multiply_convert_fusion.1
  118.0 1.6 copy-done.2
  119.6 2.8 fusion.16
  122.4 3.8 fusion.27
  126.2 2.6 copy-done.1
  129.0 3.7 fusion.28
  132.7 6.6 %copy.22 = f32[24,256,2,128]{1,0,2,3:T(8,128)} copy(f32[24,256,2,128]{3,1,2,0:T(8,128)} %fusion.28) | data formatting | bytes 12582912 | tf_op jit(solution)/shard_map/bsji,bjf->bsif/dot_general | solution.py:45
  139.4 4.4 %fusion.10 = f32[24,128,256]{2,0,1:T(8,128)S(1)} fusion(f32[24,256,2,128]{1,0,2,3:T(8,128)} %copy.22, s32[24,2]{0,1:T(2,128)S(1)} %copy-done.5, pred[24,2]{0,1:T(4,128)(4,1)S(1)} %get-tuple-element.5), kind=kOutput, calls=%fused_computation.21 | convolution fusion | flops 452987136 | bytes 9437424 | tf_op jit(solution)/shard_map/cbs,bsif->cif/dot_general | solution.py:50
  143.8 2.7 copy.19
  146.5 4.3 %fusion.3 = bf16[3072,256]{1,0:T(8,128)(2,1)} fusion(f32[3072,512]{1,0:T(8,128)} %copy-done.1, f32[24,128,256]{2,1,0:T(8,128)} %copy.19), kind=kLoop, calls=%fused_computation.12 | loop fusion | flops 1572864 | bytes 7864320 | tf_op jit(solution)/shard_map/convert_element_type | solution.py:53
  150.8 255.8 %all-reduce.3.cloned.1.call-done = (f32[512,512]{1,0:T(8,128)}, f32[512,256]{1,0:T(8,128)}) async-done(((f32[512,512]{1,0:T(8,128)}, f32[512,256]{1,0:T(8,128)}), (f32[512,512]{1,0:T(8,128)}, f32[512,256]{1,0:T(8,128)})) %all-reduce.3.cloned.1.call-update) | async-done | bytes 1572880 | tf_op jit(solution)/shard_map/psum | solution.py:60
  406.6 1.3 constant_dynamic-slice_fusion.1
  407.9 1.3 constant_dynamic-slice_fusion
  (23 shorter events, 0.6 us)
Async XLA Ops:
  7.2 101.0 %copy-start = (bf16[24,2,128,128]{3,2,1,0:T(8,128)(2,1)S(1)}, bf16[24,2,128,128]{3,2,1,0:T(8,128)(2,1)}, u32[]{:S(2)}) copy-start(bf16[24,2,128,128]{3,2,1,0:T(8,128)(2,1)} %param.11) | copy-start | bytes 4718596
  7.2 88.8 %all-gather.2.cloned.1.call-start = ((), (), s32[]{:S(2)}) async-start(), calls=%async_computation | async-start | bytes 8519680 | tf_op jit(solution)/shard_map/all_gather | solution.py:20
  9.0 397.6 %all-reduce.3.cloned.1.call-start = ((), (), s32[]{:S(2)}) async-start(), calls=%async_computation.1 | async-start | bytes 3145728 | tf_op jit(solution)/shard_map/psum | solution.py:60
  96.0 3.9 copy-start.3
  108.1 2.6 copy-start.4
  110.8 1.8 copy-start.6
  112.6 2.6 copy-start.7
  118.0 1.6 copy-start.2
  126.2 2.6 copy-start.1
  132.7 6.6 %copy-start.5 = (s32[24,2]{0,1:T(2,128)S(1)}, s32[24,2]{0,1:T(2,128)}, u32[]{:S(2)}) copy-start(s32[24,2]{0,1:T(2,128)} %param.12) | copy-start | bytes 580
Sparse Core Ops, SparseCore 0:
  11.3 84.6 all-gather.1
  146.6 259.9 all-reduce.2
where the time goes:
time: 416 us
  waiting for transfers between devices  340 us (82%)
  matrix products  24.4 us (6%)
  local copies, waits for them, and re-layouts  21.9 us (5%)
  other arithmetic  15 us (4%)
  between operations  14.2 us (3%)
    psum x1, waiting for transfers between devices, local(): lax.psum((jnp.einsum('nc,nh->ch', joined, grad_preact, preferred_element_...  256 us
    all_gather x1, waiting for transfers between devices, local(): lax.all_gather(cache_copy, 'dom', axis=0, tiled=True)  84.6 us
  transfers between devices with their start and end apart: 2, of which 2 were waited for; matrix products, arithmetic and copies ran while one was open for 2% of the time, Pallas kernels for 0%

commit v1 on v0

--- a/solution.py
+++ b/solution.py
@@ -58,13 +58,16 @@
     rows_in = weight_in.shape[0] // partners
     rows_out = weight_out.shape[0] // partners
     summed = lax.psum(
-        (
-            jnp.einsum("nc,nh->ch", joined, grad_preact, preferred_element_type=jnp.float32)
-            * loss_scale,
-            jnp.einsum("nh,nf->hf", hidden, cotangent, preferred_element_type=jnp.float32)
-            * loss_scale,
+        lax.psum(
+            (
+                jnp.einsum("nc,nh->ch", joined, grad_preact, preferred_element_type=jnp.float32)
+                * loss_scale,
+                jnp.einsum("nh,nf->hf", hidden, cotangent, preferred_element_type=jnp.float32)
+                * loss_scale,
+            ),
+            "dom",
         ),
-        ("grp", "dom"),
+        "grp",
     )
     position = lax.axis_index("dom")
     grad_weight_in = lax.dynamic_slice_in_dim(summed[0], position * rows_in, rows_in, 0)

time: 416 us -> 377 us (0.906)
  waiting for transfers between devices: 340 us -> 303 us
    psum x1, waiting for transfers between devices: 256 us -> 181 us  [local(): lax.psum((jnp.einsum('nc,nh->ch', joined, grad_preact, preferred_element_...]
    psum x0 -> x1, waiting for transfers between devices: none -> 37.9 us  [local(): lax.psum(lax.psum((jnp.einsum('nc,nh->ch', joined, grad_preact, preferred...]
  transfers between devices with their start and end apart: 2 -> 3, of which waited for: 2 -> 3; matrix products, arithmetic and copies ran while one was open for 2% -> 7% of each run, Pallas kernels for 0% -> 0%
where the time goes in v1:
time: 377 us; the launch traced here: 376 us
  waiting for transfers between devices  303 us (80%)
  matrix products  24.4 us (6%)
  local copies, waits for them, and re-layouts  20.4 us (5%)
  other arithmetic  14.1 us (4%)
  between operations  13.9 us (4%)
    psum x1, waiting for transfers between devices, local(): lax.psum((jnp.einsum('nc,nh->ch', joined, grad_preact, preferred_element_...  181 us
    all_gather x1, waiting for transfers between devices, local(): lax.all_gather(cache_copy, 'dom', axis=0, tiled=True)  84.7 us
    psum x1, waiting for transfers between devices, local(): lax.psum(lax.psum((jnp.einsum('nc,nh->ch', joined, grad_preact, preferred...  37.9 us
  transfers between devices with their start and end apart: 3, of which 3 were waited for; matrix products, arithmetic and copies ran while one was open for 7% of the time, Pallas kernels for 0%

profile of v1, /device:TPU:2, one launch (start us, length us, event | category | flops | bytes accessed | tf_op | source)
XLA Modules:
  0.0 376.3 jit_solution(17169981892298824667)
XLA Ops:
  7.2 1.7 convert_element_type.20
  9.0 0.7 compare_and_fusion
  9.8 0.7 compare_select_fusion
  11.4 84.7 %all-gather.2.cloned.1.call-done = bf16[16384,256]{1,0:T(8,128)(2,1)} async-done(((bf16[256,256]{1,0:T(8,128)(2,1)}), bf16[16384,256]{1,0:T(8,128)(2,1)}) %all-gather.2.cloned.1.call-update) | async-done | bytes 8388624 | tf_op jit(solution)/shard_map/all_gather | solution.py:20
  96.0 3.9 %fusion.2 = bf16[64,128,256]{2,1,0:T(8,128)(2,1)S(1)} fusion(bf16[64,2,128,256]{3,2,1,0:T(8,128)(2,1)} %bitcast.49, pred[64]{0:T(512)(128)(4,1)S(1)} %compare_bitcast_fusion), kind=kLoop, calls=%fused_computation.8 | loop fusion | flops 2097152 | bytes 12582976 | tf_op jit(solution)/shard_map/jit(_where)/select_n | solution.py:25
  99.9 3.0 pad_maximum_fusion
  102.9 5.2 %gather_fusion = bf16[48,128,256]{2,1,0:T(8,128)(2,1)} fusion(bf16[88,128,256]{2,1,0:T(8,128)(2,1)} %pad_maximum_fusion, s32[1024]{0:T(1024)S(1)} %pad_clamp_fusion), kind=kCustom, calls=%fused_computation | custom fusion | bytes 6291648 | tf_op jit(solution)/shard_map/gather | solution.py:29
  108.1 2.6 bitcast_convert_fusion
  110.8 1.8 fusion.9
  112.6 2.6 fusion.17
  115.2 2.7 multiply_convert_fusion.1
  118.0 1.6 copy-done.2
  119.6 2.8 fusion.16
  122.6 3.8 %fusion.27 = f32[3072,512]{1,0:T(8,128)S(1)} fusion(bf16[3072,512]{1,0:T(8,128)(2,1)} %copy-done.2, bf16[512,512]{1,0:T(8,128)(2,1)} %param.15), kind=kOutput, calls=%fused_computation.41 | convolution fusion | flops 1610612736 | bytes 9961472 | tf_op jit(solution)/shard_map/nh,ch->nc/dot_general | solution.py:39
  126.5 2.7 copy-done.1
  129.3 180.6 %all-reduce.5.cloned.1.call-done = (f32[512,512]{1,0:T(8,128)}, f32[512,256]{1,0:T(8,128)}) async-done(((f32[512,512]{1,0:T(8,128)}, f32[512,256]{1,0:T(8,128)}), (f32[512,512]{1,0:T(8,128)}, f32[512,256]{1,0:T(8,128)})) %all-reduce.5.cloned.1.call-update) | async-done | bytes 1572880 | tf_op jit(solution)/shard_map/psum | solution.py:61
  310.0 3.7 fusion.28
  313.6 6.7 %copy.22 = f32[24,256,2,128]{1,0,2,3:T(8,128)} copy(f32[24,256,2,128]{3,1,2,0:T(8,128)} %fusion.28) | data formatting | bytes 12582912 | tf_op jit(solution)/shard_map/bsji,bjf->bsif/dot_general | solution.py:45
  320.4 4.4 %fusion.10 = f32[24,128,256]{2,0,1:T(8,128)S(1)} fusion(f32[24,256,2,128]{1,0,2,3:T(8,128)} %copy.22, s32[24,2]{0,1:T(2,128)S(1)} %copy-done.5, pred[24,2]{0,1:T(4,128)(4,1)S(1)} %get-tuple-element.7), kind=kOutput, calls=%fused_computation.21 | convolution fusion | flops 452987136 | bytes 9437424 | tf_op jit(solution)/shard_map/cbs,bsif->cif/dot_general | solution.py:50
  324.8 1.0 copy.19
  325.8 3.5 fusion.3
  329.3 37.9 %all-reduce.7.cloned.1.call-done = (f32[512,512]{1,0:T(8,128)}, f32[512,256]{1,0:T(8,128)}) async-done(((f32[512,512]{1,0:T(8,128)}, f32[512,256]{1,0:T(8,128)}), (f32[512,512]{1,0:T(8,128)}, f32[512,256]{1,0:T(8,128)})) %all-reduce.7.cloned.1.call-update) | async-done | bytes 1572880 | tf_op jit(solution)/shard_map/psum | solution.py:60
  367.2 1.3 constant_dynamic-slice_fusion.1
  368.5 1.3 constant_dynamic-slice_fusion
  (26 shorter events, 1.5 us)
Async XLA Ops:
  7.2 101.0 %copy-start = (bf16[24,2,128,128]{3,2,1,0:T(8,128)(2,1)S(1)}, bf16[24,2,128,128]{3,2,1,0:T(8,128)(2,1)}, u32[]{:S(2)}) copy-start(bf16[24,2,128,128]{3,2,1,0:T(8,128)(2,1)} %param.11) | copy-start | bytes 4718596
  7.2 88.8 %all-gather.2.cloned.1.call-start = ((), (), s32[]{:S(2)}) async-start(), calls=%async_computation | async-start | bytes 8519680 | tf_op jit(solution)/shard_map/all_gather | solution.py:20
  9.0 301.0 %all-reduce.5.cloned.1.call-start = ((), (), s32[]{:S(2)}) async-start(), calls=%async_computation.1 | async-start | bytes 3145728 | tf_op jit(solution)/shard_map/psum | solution.py:61
  96.0 3.9 %copy-start.3 = (bf16[3072,256]{1,0:T(8,128)(2,1)S(1)}, bf16[3072,256]{1,0:T(8,128)(2,1)}, u32[]{:S(2)}) copy-start(bf16[3072,256]{1,0:T(8,128)(2,1)} %param.9) | copy-start | bytes 4718596
  108.1 2.6 copy-start.4
  110.8 1.8 copy-start.6
  112.6 2.6 copy-start.7
  117.9 1.7 copy-start.2
  122.4 244.7 %all-reduce.7.cloned.1.call-start = ((), (), s32[]{:S(2)}) async-start(), calls=%async_computation.2 | async-start | bytes 3145728 | tf_op jit(solution)/shard_map/psum | solution.py:60
  126.5 2.7 copy-start.1
  313.6 6.7 %copy-start.5 = (s32[24,2]{0,1:T(2,128)S(1)}, s32[24,2]{0,1:T(2,128)}, u32[]{:S(2)}) copy-start(s32[24,2]{0,1:T(2,128)} %param.12) | copy-start | bytes 580
Sparse Core Ops, SparseCore 0:
  11.3 84.6 all-gather.1
  122.5 187.3 all-reduce.4
  312.5 54.6 all-reduce.6
